TPU v7x, 32 devices: a whole 2x2x4 slice. The times are simulated.
32 devices in a mesh: outer: 8 (over z, x), inner: 4 (over y, core).
Axes of the slice: x: 2, y: 2, z: 4, core: 2. Of those that a mesh axis runs over, the one named last changes fastest.
Arguments:
- state_vector: float32 [2, 8, 4, 32768], P(None, 'outer', 'inner'), may hold values from -6 to 6
- gate_matrices: float32 [4, 2, 128, 128], replicated, may hold values from -4 to 4, as said below
Outputs:
- final_state: float32 [2, 8, 4, 32768], P(None, 'outer', 'inner')
- state_rms: float32 [], replicated
Inputs may be any that keep to these rules, and one draw needn't show every extreme that they name: `gate_matrices`: each gate is a general complex matrix, not necessarily unitary.
All inputs are finite; a program needn't handle non-finite values.
Results may differ from a plain program's by a relative error of at most 0.000098.
Values sent between devices are 32-bit elements; how exact they have to be, the bound alone decides.
A program may use at most 64 MiB of HBM per device.

v0:
```python
import jax
import jax.numpy as jnp
from jax import lax
from jax.sharding import PartitionSpec as P


def rows_apply(matrix_pair, blocks):

    def product(gate_matrix, value_entries):
        return jnp.einsum(
            "ng,wgy->wny", gate_matrix, value_entries, precision=lax.Precision.HIGHEST
        )

    real_out = product(matrix_pair[0], blocks[0]) - product(matrix_pair[1], blocks[1])
    imag_out = product(matrix_pair[0], blocks[1]) + product(matrix_pair[1], blocks[0])
    return jnp.stack([real_out, imag_out])


def low_gate(amplitude_values, matrix_pair):
    gate_dim = matrix_pair.shape[1]
    blocks = amplitude_values.reshape(2, -1, gate_dim)

    def product(gate_matrix, value_entries):
        return jnp.dot(value_entries, gate_matrix.T, precision=lax.Precision.HIGHEST)

    real_out = product(matrix_pair[0], blocks[0]) - product(matrix_pair[1], blocks[1])
    imag_out = product(matrix_pair[0], blocks[1]) + product(matrix_pair[1], blocks[0])
    return jnp.stack([real_out, imag_out]).reshape(amplitude_values.shape)


def gate_block(matrix_pair, portion):
    gate_dim = matrix_pair.shape[1]
    flat_view = portion.reshape(2, 1, gate_dim, -1)
    return rows_apply(matrix_pair, flat_view).reshape(portion.shape)


def trade_outer(blocks, mapper):
    return mapper(lax.all_to_all(blocks, "outer", split_axis=1, concat_axis=1, tiled=True))


def trade_inner(blocks, mapper):
    return mapper(lax.all_to_all(blocks, "inner", split_axis=1, concat_axis=1, tiled=True))


def shards(state_vector, gate_matrices):
    amp_count = state_vector.shape[3]
    gate_dim = gate_matrices.shape[2]
    amplitude_values = state_vector.reshape(2, amp_count)
    amplitude_values = rows_apply(
        gate_matrices[0], amplitude_values.reshape(2, -1, gate_dim, gate_dim)
    ).reshape(2, amp_count)
    outer_count = lax.axis_size("outer")
    blocks = amplitude_values.reshape(
        2, outer_count, gate_dim // outer_count, amp_count // gate_dim
    )
    blocks = trade_outer(blocks, lambda portion: gate_block(gate_matrices[1], portion))
    amplitude_values = trade_outer(blocks, lambda portion: portion).reshape(2, amp_count)
    inner_count = lax.axis_size("inner")
    blocks = amplitude_values.reshape(
        2, inner_count, gate_dim // inner_count, amp_count // gate_dim
    )
    blocks = trade_inner(blocks, lambda portion: gate_block(gate_matrices[2], portion))
    amplitude_values = trade_inner(blocks, lambda portion: portion).reshape(2, amp_count)
    amplitude_values = low_gate(amplitude_values, gate_matrices[3])
    partial_sum = jnp.sum(amplitude_values * amplitude_values)
    total_sum = lax.psum(partial_sum, ("outer", "inner"))
    amplitude_total = amp_count * lax.axis_size("outer") * inner_count
    root_mean = jnp.sqrt(total_sum / amplitude_total)
    final_state = (amplitude_values / root_mean).reshape(2, 1, 1, amp_count)
    return (final_state, root_mean)


def solution(mesh):
    in_specs = (P(None, "outer", "inner", None), P())
    out_specs = (P(None, "outer", "inner", None), P())
    return jax.shard_map(shards, mesh=mesh, in_specs=in_specs, out_specs=out_specs, check_vma=False)
```

profile of v0, /device:TPU:0, one launch (start us, length us, event | category | flops | bytes accessed | tf_op | source)
XLA Modules:
  0.0 94.8 jit_solution(15729318179131425875)
XLA Ops:
  0.6 0.0 copy-start
  0.6 1.0 %fusion.46 = (f32[1,1,1,32768]{3,2,1,0:T(1,128)S(1)}, f32[1,1,1,32768]{3,2,1,0:T(1,128)S(1)}) fusion(f32[2,1,1,32768]{3,2,1,0:T(1,128)} %param.2), kind=kLoop, calls=%fused_computation.59 | loop fusion | bytes 524288 | tf_op jit(solution)/shard_map/slice | solution.py:14
  1.7 0.1 copy-done
  1.8 0.4 fusion.23
  2.2 0.4 fusion.25
  2.6 0.4 fusion
  3.0 0.4 fusion.1
  3.4 0.1 copy.23
  3.5 0.1 copy.26
  3.7 16.0 %all_to_all.20 = f32[2,8,16,256]{3,2,0,1:T(8,128)S(1)} all-to-all(f32[2,8,16,256]{3,2,0,1:T(8,128)S(1)} %copy.27), channel_id=1, replica_groups=mesh['outer'=8,'inner'=4] {'outer'}, dimensions={1} | all-to-all | bytes 524288 | tf_op jit(solution)/shard_map/all_to_all | solution.py:38
  19.7 0.3 fusion.17
  20.0 0.3 fusion.19
  20.3 0.3 convolution_add_fusion.2
  20.6 0.3 convolution_subtract_fusion.2
  20.9 12.0 %all_to_all.21 = f32[2,8,16,256]{3,2,0,1:T(8,128)S(1)} all-to-all(f32[2,8,16,256]{3,2,0,1:T(8,128)S(1)} %pad_maximum_fusion.1), channel_id=1, replica_groups=mesh['outer'=8,'inner'=4] {'outer'}, dimensions={1} | all-to-all | bytes 524288 | tf_op jit(solution)/shard_map/all_to_all | solution.py:38
  32.9 8.6 %all_to_all.22 = f32[2,4,32,256]{3,2,0,1:T(8,128)S(1)} all-to-all(f32[2,4,32,256]{3,2,0,1:T(8,128)S(1)} %copy.31), channel_id=1, replica_groups=mesh['outer'=8,'inner'=4] {'inner'}, dimensions={1} | all-to-all | bytes 524288 | tf_op jit(solution)/shard_map/all_to_all | solution.py:42
  41.5 0.3 fusion.11
  41.8 0.3 fusion.13
  42.1 0.3 convolution_add_fusion.1
  42.3 0.3 convolution_subtract_fusion.1
  42.6 8.4 %all_to_all.23 = f32[2,4,32,256]{3,2,0,1:T(8,128)S(1)} all-to-all(f32[2,4,32,256]{3,2,0,1:T(8,128)S(1)} %pad_maximum_fusion.2), channel_id=1, replica_groups=mesh['outer'=8,'inner'=4] {'inner'}, dimensions={1} | all-to-all | bytes 524288 | tf_op jit(solution)/shard_map/all_to_all | solution.py:42
  51.1 0.3 fusion.5
  51.4 0.3 fusion.7
  51.7 0.3 convolution_add_fusion
  52.0 0.3 convolution_subtract_fusion
  52.2 0.9 fusion.2
  53.1 38.9 %psum.7 = f32[]{:T(128)} all-reduce(f32[]{:T(128)} %fusion.2), channel_id=1, replica_groups=mesh['outer'=8,'inner'=4] {'outer','inner'}, use_global_device_ids=true, to_apply=%region_1.0 | all-reduce | flops 1 | bytes 8 | tf_op jit(solution)/shard_map/psum | solution.py:66
  92.8 0.9 maximum_divide_fusion
  (13 shorter events, 0.3 us)
Async XLA Ops:
  0.6 1.2 %copy-start = (f32[4,2,128,128]{3,2,1,0:T(8,128)S(1)}, f32[4,2,128,128]{3,2,1,0:T(8,128)}, u32[]{:S(2)}) copy-start(f32[4,2,128,128]{3,2,1,0:T(8,128)} %param.3) | copy-start | bytes 1572868
where the time goes:
time: 95.3 us; the launch traced here: 94.8 us
  blocking collectives  83.9 us (88%)
  matrix products  4.82 us (5%)
  between operations  2.7 us (3%)
  other arithmetic  1.86 us (2%)
  local copies, waits for them, and re-layouts  1.55 us (2%)
    psum x1, blocking collectives, shards(): total_sum = lax.psum(partial_sum, ('outer', 'inner'))  38.9 us
    all_to_all x2, blocking collectives, trade_outer(): lax.all_to_all(blocks, 'outer', split_axis=1, concat_axis=1, tiled=True)  28 us
    all_to_all x2, blocking collectives, trade_inner(): lax.all_to_all(blocks, 'inner', split_axis=1, concat_axis=1, tiled=True)  17 us
    dot_general x12, matrix products, product(): jnp.einsum('ng,wgy->wny', gate_matrix, value_entries, precision=lax.Preci...  3.71 us

commit v1 on v0

v1 whole, which is shorter than its diff:
```python
import functools

import jax
import jax.numpy as jnp
from jax import lax
from jax.experimental import pallas as pl
from jax.experimental.pallas import tpu as pltpu
from jax.sharding import PartitionSpec as P

MESH = pl.DeviceIdType.MESH


def halves(values):
    high = values.astype(jnp.bfloat16)
    low = (values - high.astype(jnp.float32)).astype(jnp.bfloat16)
    return high, low


def product(left, right, dims):
    def one(a, b):
        return lax.dot_general(a, b, (dims, ((), ())), preferred_element_type=jnp.float32)

    return one(left[0], right[0]) + (one(left[0], right[1]) + one(left[1], right[0]))


def complex_matrix(real, imag):
    top = jnp.concatenate([real, -imag], axis=1)
    bottom = jnp.concatenate([imag, real], axis=1)
    return halves(jnp.concatenate([top, bottom], axis=0))


def spread(position, count):
    return (position % 2) * (count // 2) + position // 2


def kernel(
    n_outer, n_inner, chunks, state, gates, out, rms,
    sent_a, held_a, sent_b, held_b, sent_c, held_c, part, sums,
    send_a, recv_a, send_b, recv_b, send_c, recv_c, send_s, recv_s,
):
    dim = gates.shape[2]
    passive = state.shape[1] // dim
    sub = passive // chunks
    step = dim // chunks
    rows_outer = dim // n_outer * sub
    rows_inner = dim // n_inner * sub
    ratio = n_outer // n_inner
    n_all = n_outer * n_inner
    outer, inner = lax.axis_index("outer"), lax.axis_index("inner")
    me = outer * n_inner + inner

    def block(ref, chunk, at, rows):
        return ref.at[chunk, :, pl.ds(pl.multiple_of(at * rows, rows), rows), :]

    def remote(src, dst, send, recv, target):
        return pltpu.make_async_remote_copy(
            src_ref=src, dst_ref=dst, send_sem=send, recv_sem=recv,
            device_id=target, device_id_type=MESH,
        )

    def everyone(act):
        def body(k, carry):
            peer = (me + k) % n_all
            act(k, peer, (peer // n_inner, peer % n_inner))
            return carry

        lax.fori_loop(1, n_all, body, 0)

    barrier = pltpu.get_barrier_semaphore()

    def greet(k, peer, target):
        pl.semaphore_signal(barrier, inc=1, device_id=target, device_id_type=MESH)

    everyone(greet)

    def load(ref, chunk):
        return jnp.concatenate(
            [
                jnp.concatenate(
                    [ref[chunk, c, pl.ds(b, dim, stride=sub), :] for b in range(sub)], axis=1
                )
                for c in range(2)
            ],
            axis=0,
        )

    def store(ref, chunk, values):
        for c in range(2):
            for b in range(sub):
                ref[chunk, c, pl.ds(b, dim, stride=sub), :] = values[
                    c * dim : (c + 1) * dim, b * dim : (b + 1) * dim
                ]

    def low_gate(matrix, values):
        columns = []
        for b in range(sub):
            both = values[:, b * dim : (b + 1) * dim]
            wide = jnp.concatenate([both[:dim], both[dim:]], axis=1)
            wide = product(halves(wide), matrix, ((1,), (1,)))
            columns.append(jnp.concatenate([wide[:, :dim], wide[:, dim:]], axis=0))
        return jnp.concatenate(columns, axis=1)

    first = halves(
        jnp.concatenate(
            [
                jnp.concatenate(
                    [state[c, w * dim : (w + 1) * dim, :] for w in range(passive)], axis=1
                )
                for c in range(2)
            ],
            axis=0,
        )
    )

    def trade_a(chunk):
        for k in range(1, n_outer):
            to = (outer + k) % n_outer
            remote(
                block(sent_a, chunk, spread(to, n_outer), rows_outer),
                block(held_a, chunk, outer, rows_outer),
                send_a.at[chunk, to], recv_a.at[chunk, outer], (to, inner),
            ).start()
        pltpu.make_async_copy(
            block(sent_a, chunk, spread(outer, n_outer), rows_outer),
            block(held_a, chunk, outer, rows_outer),
            recv_a.at[chunk, outer],
        ).start()

    for chunk in range(chunks):
        pick = pl.ds(chunk, step, stride=chunks)
        matrix = complex_matrix(gates[0, 0, pick, :], gates[0, 1, pick, :])
        values = product(matrix, first, ((1,), (0,)))
        for c in range(2):
            for w in range(passive):
                sent_a[chunk, c, w * step : (w + 1) * step, :] = values[
                    c * step : (c + 1) * step, w * dim : (w + 1) * dim
                ]
        if chunk == 0:
            pl.semaphore_wait(barrier, n_all - 1)
        trade_a(chunk)

    low_matrix = complex_matrix(gates[3, 0], gates[3, 1])
    matrix = complex_matrix(gates[1, 0], gates[1, 1])
    mine = spread(outer, n_outer)
    column, within = mine // ratio, mine % ratio
    slot = inner * ratio + within
    for chunk in range(chunks):
        for k in range(n_outer):
            spot = block(held_a, chunk, k, rows_outer)
            remote(spot, spot, send_a.at[chunk, k], recv_a.at[chunk, k], (outer, inner)).wait_recv()
        values = low_gate(low_matrix, load(held_a, chunk))
        store(sent_b, chunk, product(matrix, halves(values), ((1,), (0,))))
        for k in range(n_outer):
            to = (outer + k) % n_outer
            src = block(sent_b, chunk, to, rows_outer)
            dst = block(held_b, chunk, slot, rows_outer)
            copy = remote(
                src, dst, send_b.at[chunk, to], recv_b.at[chunk, slot], (to, column)
            )
            if k > 0:
                copy.start()
            else:
                pl.when(column != inner)(copy.start)
                pl.when(column == inner)(
                    pltpu.make_async_copy(src, dst, recv_b.at[chunk, slot]).start
                )

    matrix = complex_matrix(gates[2, 0], gates[2, 1])
    total = jnp.zeros((8, dim), jnp.float32)
    for chunk in range(chunks):
        for k in range(n_outer):
            spot = block(held_b, chunk, k, rows_outer)
            remote(spot, spot, send_b.at[chunk, k], recv_b.at[chunk, k], (outer, inner)).wait_recv()
        values = product(matrix, halves(load(held_b, chunk)), ((1,), (0,)))
        store(sent_c, chunk, values)
        for k in range(1, n_inner):
            to = (inner + k) % n_inner
            remote(
                block(sent_c, chunk, to, rows_inner),
                block(held_c, chunk, inner, rows_inner),
                send_c.at[chunk, to], recv_c.at[chunk, inner], (outer, to),
            ).start()
        pltpu.make_async_copy(
            block(sent_c, chunk, inner, rows_inner),
            block(held_c, chunk, inner, rows_inner),
            recv_c.at[chunk, inner],
        ).start()
        for b in range(sub):
            piece = values[:, b * dim : (b + 1) * dim]
            total = total + jnp.sum((piece * piece).reshape(-1, 8, dim), axis=0)

    part[...] = total
    sums[me] = total

    def share(k, peer, target):
        remote(part, sums.at[me], send_s.at[k], recv_s.at[k], target).start()

    everyone(share)

    def arrived(k, peer, target):
        remote(part, sums.at[me], send_s.at[k], recv_s.at[k], target).wait_send()
        source = (me + n_all - k) % n_all
        remote(part, sums.at[source], send_s.at[k], recv_s.at[k], target).wait_recv()

    everyone(arrived)
    whole = jnp.sum(jnp.sum(sums[...], axis=0), axis=(0, 1), keepdims=True)
    count = n_all * state.shape[1] * dim
    root = jnp.sqrt(whole / count)
    rms[...] = root
    scale = jnp.broadcast_to(root, (8, dim))
    for chunk in range(chunks):
        for k in range(n_inner):
            spot = block(held_c, chunk, k, rows_inner)
            remote(spot, spot, send_c.at[chunk, k], recv_c.at[chunk, k], (outer, inner)).wait_recv()
        for c in range(2):
            values = held_c[chunk, c].reshape(-1, 8, dim) / scale[None]
            out[c, pl.ds(chunk, dim * sub, stride=chunks), :] = values.reshape(-1, dim)

    for chunk in range(chunks):
        for k in range(1, n_outer):
            to = (outer + k) % n_outer
            spot = block(sent_a, chunk, to, rows_outer)
            remote(spot, spot, send_a.at[chunk, to], recv_a.at[chunk, to], (to, inner)).wait_send()
        for k in range(n_outer):
            to = (outer + k) % n_outer
            spot = block(sent_b, chunk, to, rows_outer)
            copy = remote(spot, spot, send_b.at[chunk, to], recv_b.at[chunk, to], (to, column))
            if k > 0:
                copy.wait_send()
            else:
                pl.when(column != inner)(copy.wait_send)
        for k in range(1, n_inner):
            to = (inner + k) % n_inner
            spot = block(sent_c, chunk, to, rows_inner)
            remote(spot, spot, send_c.at[chunk, to], recv_c.at[chunk, to], (outer, to)).wait_send()


def shards(n_outer, n_inner, state_vector, gate_matrices):
    dim = gate_matrices.shape[2]
    amp_count = state_vector.shape[3]
    rows = amp_count // dim
    passive = rows // dim
    chunks = passive if (dim // n_outer) % 8 == 0 else 1
    held = pltpu.VMEM((chunks, 2, rows // chunks, dim), jnp.float32)
    n_all = n_outer * n_inner
    dma = pltpu.SemaphoreType.DMA
    vmem = pl.BlockSpec(memory_space=pltpu.VMEM)
    final_state, root = pl.pallas_call(
        functools.partial(kernel, n_outer, n_inner, chunks),
        out_shape=(
            jax.ShapeDtypeStruct((2, rows, dim), jnp.float32),
            jax.ShapeDtypeStruct((1, 1), jnp.float32),
        ),
        in_specs=[vmem, vmem],
        out_specs=(vmem, vmem),
        scratch_shapes=[held] * 6
        + [pltpu.VMEM((8, dim), jnp.float32), pltpu.VMEM((n_all, 8, dim), jnp.float32)]
        + [dma((chunks, n_outer))] * 4
        + [dma((chunks, n_inner))] * 2
        + [dma((n_all,))] * 2,
        compiler_params=pltpu.CompilerParams(collective_id=0, has_side_effects=True),
    )(state_vector.reshape(2, rows, dim), gate_matrices)
    return final_state.reshape(state_vector.shape), root.reshape(())


def solution(mesh):
    in_specs = (P(None, "outer", "inner", None), P())
    out_specs = (P(None, "outer", "inner", None), P())
    body = functools.partial(shards, mesh.shape["outer"], mesh.shape["inner"])
    return jax.shard_map(body, mesh=mesh, in_specs=in_specs, out_specs=out_specs, check_vma=False)
```

time: 95.3 us -> 34.1 us (0.36)
  blocking collectives: 83.9 us -> 0 us
  Pallas kernels: 0 us -> 29.9 us
  matrix products: 4.82 us -> 0 us
  other arithmetic: 1.86 us -> 0 us
    all_to_all x4 -> x0, blocking collectives: 44.9 us -> none  [the longest x2 28 us: trade_outer(): lax.all_to_all(blocks, 'outer', split_axis=1, concat_axis=1, tiled=True)]
    psum x1 -> x0, blocking collectives: 38.9 us -> none  [shards(): total_sum = lax.psum(partial_sum, ('outer', 'inner'))]
    pallas_call x0 -> x1, Pallas kernels: none -> 29.9 us  [shards(): pl.pallas_call(functools.partial(kernel, n_outer, n_inner, chunks), out_s...]
    dot_general x16 -> x0, matrix products: 4.82 us -> none  [the longest x12 3.71 us: product(): jnp.einsum('ng,wgy->wny', gate_matrix, value_entries, precision=lax.Preci...]
    unnamed x2 -> x1, local copies, waits for them, and re-layouts: 0.11 us -> 1.67 us
    slice x4 -> x0, local copies, waits for them, and re-layouts: 1.1 us -> none  [the longest x3 1.08 us: rows_apply(): blocks[0]]
where the time goes in v1:
time: 34.1 us; the launch traced here: 34 us
  Pallas kernels  29.9 us (88%)
  between operations  2.4 us (7%)
  local copies, waits for them, and re-layouts  1.67 us (5%)
    pallas_call x1, Pallas kernels, shards(): pl.pallas_call(functools.partial(kernel, n_outer, n_inner, chunks), out_s...  29.9 us
    unnamed x1, local copies, waits for them, and re-layouts  1.67 us

profile of v1, /device:TPU:0, one launch (start us, length us, event | category | flops | bytes accessed | tf_op | source)
XLA Modules:
  0.0 34.0 jit_solution(6895621905993049650)
XLA Ops:
  0.6 29.9 %shard_map.41 = (f32[2,256,128]{2,1,0:T(8,128)}, f32[1,1]{1,0:T(1,128)}) custom-call(f32[2,256,128]{2,1,0:T(8,128)} %bitcast.3, f32[4,2,128,128]{3,2,1,0:T(8,128)} %gates.1), custom_call_target="tpu_custom_call" | custom-call | tf_op jit(solution)/shard_map/pallas_call | solution.py:248
  30.5 1.7 %copy.7 = f32[2,1,1,32768]{3,2,1,0:T(1,128)} copy(f32[2,1,1,32768]{3,2,1,0:T(1,128)} %bitcast.4) | data formatting | bytes 524288

commit v2 on v1

--- a/solution.py
+++ b/solution.py
@@ -8,6 +8,7 @@
 from jax.sharding import PartitionSpec as P
 
 MESH = pl.DeviceIdType.MESH
+LIMIT = 16 * 1024 * 1024
 
 
 def halves(values):
@@ -34,8 +35,8 @@
 
 
 def kernel(
-    n_outer, n_inner, chunks, state, gates, out, rms,
-    sent_a, held_a, sent_b, held_b, sent_c, held_c, part, sums,
+    n_outer, n_inner, chunks, state, gates, held_c, sums,
+    sent_a, held_a, sent_b, held_b, sent_c, part,
     send_a, recv_a, send_b, recv_b, send_c, recv_c, send_s, recv_s,
 ):
     dim = gates.shape[2]
@@ -166,12 +167,24 @@
                 )
 
     matrix = complex_matrix(gates[2, 0], gates[2, 1])
-    total = jnp.zeros((8, dim), jnp.float32)
+    total = jnp.zeros((1, dim), jnp.float32)
+    own = pltpu.make_async_copy(part, sums.at[me], recv_s.at[0])
+
+    def share(k, peer, target):
+        remote(part, sums.at[me], send_s.at[k], recv_s.at[k], target).start()
+
     for chunk in range(chunks):
         for k in range(n_outer):
             spot = block(held_b, chunk, k, rows_outer)
             remote(spot, spot, send_b.at[chunk, k], recv_b.at[chunk, k], (outer, inner)).wait_recv()
         values = product(matrix, halves(load(held_b, chunk)), ((1,), (0,)))
+        for b in range(sub):
+            piece = values[:, b * dim : (b + 1) * dim]
+            total = total + jnp.sum(piece * piece, axis=0, keepdims=True)
+        if chunk == chunks - 1:
+            part[...] = total
+            everyone(share)
+            own.start()
         store(sent_c, chunk, values)
         for k in range(1, n_inner):
             to = (inner + k) % n_inner
@@ -185,17 +198,6 @@
             block(held_c, chunk, inner, rows_inner),
             recv_c.at[chunk, inner],
         ).start()
-        for b in range(sub):
-            piece = values[:, b * dim : (b + 1) * dim]
-            total = total + jnp.sum((piece * piece).reshape(-1, 8, dim), axis=0)
-
-    part[...] = total
-    sums[me] = total
-
-    def share(k, peer, target):
-        remote(part, sums.at[me], send_s.at[k], recv_s.at[k], target).start()
-
-    everyone(share)
 
     def arrived(k, peer, target):
         remote(part, sums.at[me], send_s.at[k], recv_s.at[k], target).wait_send()
@@ -203,18 +205,11 @@
         remote(part, sums.at[source], send_s.at[k], recv_s.at[k], target).wait_recv()
 
     everyone(arrived)
-    whole = jnp.sum(jnp.sum(sums[...], axis=0), axis=(0, 1), keepdims=True)
-    count = n_all * state.shape[1] * dim
-    root = jnp.sqrt(whole / count)
-    rms[...] = root
-    scale = jnp.broadcast_to(root, (8, dim))
+    own.wait()
     for chunk in range(chunks):
         for k in range(n_inner):
             spot = block(held_c, chunk, k, rows_inner)
             remote(spot, spot, send_c.at[chunk, k], recv_c.at[chunk, k], (outer, inner)).wait_recv()
-        for c in range(2):
-            values = held_c[chunk, c].reshape(-1, 8, dim) / scale[None]
-            out[c, pl.ds(chunk, dim * sub, stride=chunks), :] = values.reshape(-1, dim)
 
     for chunk in range(chunks):
         for k in range(1, n_outer):
@@ -235,6 +230,18 @@
             remote(spot, spot, send_c.at[chunk, to], recv_c.at[chunk, to], (outer, to)).wait_send()
 
 
+def finish(n_all, values, sums, out, rms):
+    chunks, _, rows, dim = values.shape
+    whole = jnp.sum(jnp.sum(sums[...], axis=0), axis=1, keepdims=True)
+    root = jnp.sqrt(whole / (n_all * chunks * rows * dim))
+    rms[...] = root
+    scale = jnp.broadcast_to(root, (8, dim))
+    for chunk in range(chunks):
+        for c in range(2):
+            scaled = values[chunk, c].reshape(-1, 8, dim) / scale[None]
+            out[c, pl.ds(chunk, rows, stride=chunks), :] = scaled.reshape(-1, dim)
+
+
 def shards(n_outer, n_inner, state_vector, gate_matrices):
     dim = gate_matrices.shape[2]
     amp_count = state_vector.shape[3]
@@ -245,21 +252,34 @@
     n_all = n_outer * n_inner
     dma = pltpu.SemaphoreType.DMA
     vmem = pl.BlockSpec(memory_space=pltpu.VMEM)
+    anywhere = pl.BlockSpec(memory_space=pl.ANY)
+    values, sums = pl.pallas_call(
+        functools.partial(kernel, n_outer, n_inner, chunks),
+        out_shape=(
+            jax.ShapeDtypeStruct((chunks, 2, rows // chunks, dim), jnp.float32),
+            jax.ShapeDtypeStruct((n_all, 1, dim), jnp.float32),
+        ),
+        in_specs=[vmem, vmem],
+        out_specs=(anywhere, anywhere),
+        scratch_shapes=[held] * 5
+        + [pltpu.VMEM((1, dim), jnp.float32)]
+        + [dma((chunks, n_outer))] * 4
+        + [dma((chunks, n_inner))] * 2
+        + [dma((n_all,))] * 2,
+        compiler_params=pltpu.CompilerParams(
+            collective_id=0, has_side_effects=True, vmem_limit_bytes=LIMIT
+        ),
+    )(state_vector.reshape(2, rows, dim), gate_matrices)
     final_state, root = pl.pallas_call(
-        functools.partial(kernel, n_outer, n_inner, chunks),
+        functools.partial(finish, n_all),
         out_shape=(
             jax.ShapeDtypeStruct((2, rows, dim), jnp.float32),
             jax.ShapeDtypeStruct((1, 1), jnp.float32),
         ),
         in_specs=[vmem, vmem],
         out_specs=(vmem, vmem),
-        scratch_shapes=[held] * 6
-        + [pltpu.VMEM((8, dim), jnp.float32), pltpu.VMEM((n_all, 8, dim), jnp.float32)]
-        + [dma((chunks, n_outer))] * 4
-        + [dma((chunks, n_inner))] * 2
-        + [dma((n_all,))] * 2,
-        compiler_params=pltpu.CompilerParams(collective_id=0, has_side_effects=True),
-    )(state_vector.reshape(2, rows, dim), gate_matrices)
+        compiler_params=pltpu.CompilerParams(vmem_limit_bytes=LIMIT),
+    )(values, sums)
     return final_state.reshape(state_vector.shape), root.reshape(())
 
 

time: 34.1 us -> 31.4 us (0.921)
  between operations: 2.4 us -> 0.65 us
  Pallas kernels: 29.9 us -> 28.5 us
    pallas_call x1, Pallas kernels: 29.9 us -> 27.7 us  [shards(): pl.pallas_call(functools.partial(kernel, n_outer, n_inner, chunks), out_s...]
    pallas_call x0 -> x1, Pallas kernels: none -> 0.85 us  [shards(): pl.pallas_call(functools.partial(finish, n_all), out_shape=(jax.ShapeDtyp...]
    unnamed x1 -> x4, local copies, waits for them, and re-layouts: 1.67 us -> 1.98 us
where the time goes in v2:
time: 31.4 us; the launch traced here: 31.2 us
  Pallas kernels  28.5 us (91%)
  local copies, waits for them, and re-layouts  1.98 us (6%)
  between operations  0.65 us (2%)
    pallas_call x1, Pallas kernels, shards(): pl.pallas_call(functools.partial(kernel, n_outer, n_inner, chunks), out_s...  27.7 us
    unnamed x4, local copies, waits for them, and re-layouts  1.98 us
    pallas_call x1, Pallas kernels, shards(): pl.pallas_call(functools.partial(finish, n_all), out_shape=(jax.ShapeDtyp...  0.85 us

profile of v2, /device:TPU:0, one launch (start us, length us, event | category | flops | bytes accessed | tf_op | source)
XLA Modules:
  0.0 31.2 jit_solution(11613542494953450623)
XLA Ops:
  0.6 0.0 copy-start
  0.6 1.0 %copy-done = f32[4,2,128,128]{3,2,1,0:T(8,128)S(1)} copy-done((f32[4,2,128,128]{3,2,1,0:T(8,128)S(1)}, f32[4,2,128,128]{3,2,1,0:T(8,128)}, u32[]{:S(2)}) %copy-start) | copy-done | bytes 524312
  1.7 0.0 copy-start.1
  1.7 0.9 %copy-done.1 = f32[2,1,1,32768]{3,2,1,0:T(1,128)S(1)} copy-done((f32[2,1,1,32768]{3,2,1,0:T(1,128)S(1)}, f32[2,1,1,32768]{3,2,1,0:T(1,128)}, u32[]{:S(2)}) %copy-start.1) | copy-done | bytes 262168
  2.6 27.7 %shard_map.41 = (f32[2,2,128,128]{3,2,1,0:T(8,128)S(1)}, f32[32,1,128]{2,1,0:T(1,128)S(1)}) custom-call(f32[2,256,128]{2,1,0:T(8,128)S(1)} %bitcast.3, f32[4,2,128,128]{3,2,1,0:T(8,128)S(1)} %copy-done), custom_call_target="tpu_custom_call" | custom-call | tf_op jit(solution)/shard_map/pallas_call | solution.py:256
  30.3 0.8 %shard_map.42 = (f32[2,256,128]{2,1,0:T(8,128)}, f32[1,1]{1,0:T(1,128)}) custom-call(f32[2,2,128,128]{3,2,1,0:T(8,128)S(1)} %get-tuple-element.6.values, f32[32,1,128]{2,1,0:T(1,128)S(1)} %get-tuple-element.7.sums), custom_call_target="tpu_custom_call" | custom-call | tf_op jit(solution)/shard_map/pallas_call | solution.py:273
Async XLA Ops:
  0.6 1.0 %copy-start = (f32[4,2,128,128]{3,2,1,0:T(8,128)S(1)}, f32[4,2,128,128]{3,2,1,0:T(8,128)}, u32[]{:S(2)}) copy-start(f32[4,2,128,128]{3,2,1,0:T(8,128)} %gates.1) | copy-start | bytes 1572868
  1.7 0.9 %copy-start.1 = (f32[2,1,1,32768]{3,2,1,0:T(1,128)S(1)}, f32[2,1,1,32768]{3,2,1,0:T(1,128)}, u32[]{:S(2)}) copy-start(f32[2,1,1,32768]{3,2,1,0:T(1,128)} %param.2) | copy-start | bytes 786436

commit v3 on v2

--- a/solution.py
+++ b/solution.py
@@ -8,6 +8,7 @@
 from jax.sharding import PartitionSpec as P
 
 MESH = pl.DeviceIdType.MESH
+TRADE_LIMIT = 56_150_000
 LIMIT = 16 * 1024 * 1024
 
 
@@ -35,10 +36,17 @@
 
 
 def kernel(
-    n_outer, n_inner, chunks, state, gates, held_c, sums,
-    sent_a, held_a, sent_b, held_b, sent_c, part,
+    n_outer, n_inner, chunks, state_in, gates_in, held_c, sums,
+    state, gates, sent_a, held_a, sent_b, held_b, sent_c, part, fetched,
     send_a, recv_a, send_b, recv_b, send_c, recv_c, send_s, recv_s,
 ):
+    def fetch(at):
+        if at == 0:
+            return pltpu.make_async_copy(state_in, state, fetched.at[0])
+        return pltpu.make_async_copy(gates_in.at[at - 1], gates.at[at - 1], fetched.at[at])
+
+    for at in (0, 1, 4, 2, 3):
+        fetch(at).start()
     dim = gates.shape[2]
     passive = state.shape[1] // dim
     sub = passive // chunks
@@ -69,10 +77,14 @@
 
     barrier = pltpu.get_barrier_semaphore()
 
-    def greet(k, peer, target):
-        pl.semaphore_signal(barrier, inc=1, device_id=target, device_id_type=MESH)
-
-    everyone(greet)
+    for k in range(1, n_outer):
+        pl.semaphore_signal(
+            barrier, inc=1, device_id=((outer + k) % n_outer, inner), device_id_type=MESH
+        )
+    for k in range(1, n_inner):
+        pl.semaphore_signal(
+            barrier, inc=1, device_id=(outer, (inner + k) % n_inner), device_id_type=MESH
+        )
 
     def load(ref, chunk):
         return jnp.concatenate(
@@ -92,15 +104,21 @@
                     c * dim : (c + 1) * dim, b * dim : (b + 1) * dim
                 ]
 
-    def low_gate(matrix, values):
+    def low_gate(values):
+        rows = values.shape[0] // 2
+        matrix = complex_matrix(gates[3, 0], gates[3, 1])
         columns = []
-        for b in range(sub):
+        for b in range(values.shape[1] // dim):
             both = values[:, b * dim : (b + 1) * dim]
-            wide = jnp.concatenate([both[:dim], both[dim:]], axis=1)
+            wide = jnp.concatenate([both[:rows], both[rows:]], axis=1)
             wide = product(halves(wide), matrix, ((1,), (1,)))
             columns.append(jnp.concatenate([wide[:, :dim], wide[:, dim:]], axis=0))
         return jnp.concatenate(columns, axis=1)
 
+    far_first = sorted(range(n_outer), key=lambda k: abs(2 * k - n_outer))
+
+    fetch(0).wait()
+    fetch(1).wait()
     first = halves(
         jnp.concatenate(
             [
@@ -114,7 +132,7 @@
     )
 
     def trade_a(chunk):
-        for k in range(1, n_outer):
+        for k in far_first[:-1]:
             to = (outer + k) % n_outer
             remote(
                 block(sent_a, chunk, spread(to, n_outer), rows_outer),
@@ -131,16 +149,20 @@
         pick = pl.ds(chunk, step, stride=chunks)
         matrix = complex_matrix(gates[0, 0, pick, :], gates[0, 1, pick, :])
         values = product(matrix, first, ((1,), (0,)))
+        if chunk > 0:
+            if chunk == 1:
+                fetch(4).wait()
+            values = low_gate(values)
         for c in range(2):
             for w in range(passive):
                 sent_a[chunk, c, w * step : (w + 1) * step, :] = values[
                     c * step : (c + 1) * step, w * dim : (w + 1) * dim
                 ]
         if chunk == 0:
-            pl.semaphore_wait(barrier, n_all - 1)
+            pl.semaphore_wait(barrier, n_outer + n_inner - 2)
         trade_a(chunk)
 
-    low_matrix = complex_matrix(gates[3, 0], gates[3, 1])
+    fetch(2).wait()
     matrix = complex_matrix(gates[1, 0], gates[1, 1])
     mine = spread(outer, n_outer)
     column, within = mine // ratio, mine % ratio
@@ -149,9 +171,9 @@
         for k in range(n_outer):
             spot = block(held_a, chunk, k, rows_outer)
             remote(spot, spot, send_a.at[chunk, k], recv_a.at[chunk, k], (outer, inner)).wait_recv()
-        values = low_gate(low_matrix, load(held_a, chunk))
-        store(sent_b, chunk, product(matrix, halves(values), ((1,), (0,))))
-        for k in range(n_outer):
+        values = halves(load(held_a, chunk))
+        store(sent_b, chunk, product(matrix, values, ((1,), (0,))))
+        for k in far_first:
             to = (outer + k) % n_outer
             src = block(sent_b, chunk, to, rows_outer)
             dst = block(held_b, chunk, slot, rows_outer)
@@ -166,6 +188,7 @@
                     pltpu.make_async_copy(src, dst, recv_b.at[chunk, slot]).start
                 )
 
+    fetch(3).wait()
     matrix = complex_matrix(gates[2, 0], gates[2, 1])
     total = jnp.zeros((1, dim), jnp.float32)
     own = pltpu.make_async_copy(part, sums.at[me], recv_s.at[0])
@@ -178,6 +201,10 @@
             spot = block(held_b, chunk, k, rows_outer)
             remote(spot, spot, send_b.at[chunk, k], recv_b.at[chunk, k], (outer, inner)).wait_recv()
         values = product(matrix, halves(load(held_b, chunk)), ((1,), (0,)))
+        if chunk == 0:
+            if chunks == 1:
+                fetch(4).wait()
+            values = low_gate(values)
         for b in range(sub):
             piece = values[:, b * dim : (b + 1) * dim]
             total = total + jnp.sum(piece * piece, axis=0, keepdims=True)
@@ -252,6 +279,7 @@
     n_all = n_outer * n_inner
     dma = pltpu.SemaphoreType.DMA
     vmem = pl.BlockSpec(memory_space=pltpu.VMEM)
+    hbm = pl.BlockSpec(memory_space=pltpu.HBM)
     anywhere = pl.BlockSpec(memory_space=pl.ANY)
     values, sums = pl.pallas_call(
         functools.partial(kernel, n_outer, n_inner, chunks),
@@ -259,15 +287,19 @@
             jax.ShapeDtypeStruct((chunks, 2, rows // chunks, dim), jnp.float32),
             jax.ShapeDtypeStruct((n_all, 1, dim), jnp.float32),
         ),
-        in_specs=[vmem, vmem],
+        in_specs=[hbm, hbm],
         out_specs=(anywhere, anywhere),
-        scratch_shapes=[held] * 5
-        + [pltpu.VMEM((1, dim), jnp.float32)]
+        scratch_shapes=[
+            pltpu.VMEM((2, rows, dim), jnp.float32),
+            pltpu.VMEM(gate_matrices.shape, jnp.float32),
+        ]
+        + [held] * 5
+        + [pltpu.VMEM((1, dim), jnp.float32), dma((5,))]
         + [dma((chunks, n_outer))] * 4
         + [dma((chunks, n_inner))] * 2
         + [dma((n_all,))] * 2,
         compiler_params=pltpu.CompilerParams(
-            collective_id=0, has_side_effects=True, vmem_limit_bytes=LIMIT
+            collective_id=0, has_side_effects=True, vmem_limit_bytes=TRADE_LIMIT
         ),
     )(state_vector.reshape(2, rows, dim), gate_matrices)
     final_state, root = pl.pallas_call(

time: 31.4 us -> 27.5 us (0.88)
  local copies, waits for them, and re-layouts: 1.98 us -> 0 us
  Pallas kernels: 28.5 us -> 26.7 us
    unnamed x4 -> x0, local copies, waits for them, and re-layouts: 1.98 us -> none
    pallas_call x1, Pallas kernels: 27.7 us -> 25.8 us  [shards(): pl.pallas_call(functools.partial(kernel, n_outer, n_inner, chunks), out_s...]
where the time goes in v3:
time: 27.5 us; the launch traced here: 27.3 us
  Pallas kernels  26.7 us (97%)
  between operations  0.64 us (2%)
    pallas_call x1, Pallas kernels, shards(): pl.pallas_call(functools.partial(kernel, n_outer, n_inner, chunks), out_s...  25.8 us
    pallas_call x1, Pallas kernels, shards(): pl.pallas_call(functools.partial(finish, n_all), out_shape=(jax.ShapeDtyp...  0.85 us

profile of v3, /device:TPU:0, one launch (start us, length us, event | category | flops | bytes accessed | tf_op | source)
XLA Modules:
  0.0 27.3 jit_solution(3753029883998474877)
XLA Ops:
  0.6 25.8 %shard_map.41 = (f32[2,2,128,128]{3,2,1,0:T(8,128)S(1)}, f32[32,1,128]{2,1,0:T(1,128)S(1)}) custom-call(f32[2,256,128]{2,1,0:T(8,128)} %bitcast.3, f32[4,2,128,128]{3,2,1,0:T(8,128)} %gates_in.1), custom_call_target="tpu_custom_call" | custom-call | tf_op jit(solution)/shard_map/pallas_call | solution.py:284
  26.5 0.8 %shard_map.42 = (f32[2,256,128]{2,1,0:T(8,128)}, f32[1,1]{1,0:T(1,128)}) custom-call(f32[2,2,128,128]{3,2,1,0:T(8,128)S(1)} %get-tuple-element.6.values, f32[32,1,128]{2,1,0:T(1,128)S(1)} %get-tuple-element.7.sums), custom_call_target="tpu_custom_call" | custom-call | tf_op jit(solution)/shard_map/pallas_call | solution.py:305

commit v4 on v3

--- a/solution.py
+++ b/solution.py
@@ -67,13 +67,26 @@
             device_id=target, device_id_type=MESH,
         )
 
+    far_first = sorted(range(n_outer), key=lambda k: abs(2 * k - n_outer))
+
     def everyone(act):
-        def body(k, carry):
-            peer = (me + k) % n_all
-            act(k, peer, (peer // n_inner, peer % n_inner))
-            return carry
-
-        lax.fori_loop(1, n_all, body, 0)
+        if n_all > 64:
+
+            def body(k, carry):
+                one(act, k // n_inner, k % n_inner)
+                return carry
+
+            lax.fori_loop(1, n_all, body, 0)
+            return
+        for a in far_first:
+            for b in range(n_inner):
+                if a or b:
+                    one(act, a, b)
+
+    def one(act, a, b):
+        ahead = ((outer + a) % n_outer, (inner + b) % n_inner)
+        behind = ((outer + n_outer - a) % n_outer, (inner + n_inner - b) % n_inner)
+        act(a * n_inner + b, ahead, behind)
 
     barrier = pltpu.get_barrier_semaphore()
 
@@ -114,8 +127,6 @@
             wide = product(halves(wide), matrix, ((1,), (1,)))
             columns.append(jnp.concatenate([wide[:, :dim], wide[:, dim:]], axis=0))
         return jnp.concatenate(columns, axis=1)
-
-    far_first = sorted(range(n_outer), key=lambda k: abs(2 * k - n_outer))
 
     fetch(0).wait()
     fetch(1).wait()
@@ -193,8 +204,8 @@
     total = jnp.zeros((1, dim), jnp.float32)
     own = pltpu.make_async_copy(part, sums.at[me], recv_s.at[0])
 
-    def share(k, peer, target):
-        remote(part, sums.at[me], send_s.at[k], recv_s.at[k], target).start()
+    def share(k, ahead, behind):
+        remote(part, sums.at[me], send_s.at[k], recv_s.at[k], ahead).start()
 
     for chunk in range(chunks):
         for k in range(n_outer):
@@ -226,13 +237,13 @@
             recv_c.at[chunk, inner],
         ).start()
 
-    def arrived(k, peer, target):
-        remote(part, sums.at[me], send_s.at[k], recv_s.at[k], target).wait_send()
-        source = (me + n_all - k) % n_all
-        remote(part, sums.at[source], send_s.at[k], recv_s.at[k], target).wait_recv()
-
-    everyone(arrived)
-    own.wait()
+    def arrived(k, ahead, behind):
+        spot = sums.at[behind[0] * n_inner + behind[1]]
+        remote(part, spot, send_s.at[k], recv_s.at[k], ahead).wait_recv()
+
+    def left(k, ahead, behind):
+        remote(part, sums.at[me], send_s.at[k], recv_s.at[k], ahead).wait_send()
+
     for chunk in range(chunks):
         for k in range(n_inner):
             spot = block(held_c, chunk, k, rows_inner)
@@ -255,6 +266,9 @@
             to = (inner + k) % n_inner
             spot = block(sent_c, chunk, to, rows_inner)
             remote(spot, spot, send_c.at[chunk, to], recv_c.at[chunk, to], (outer, to)).wait_send()
+    everyone(left)
+    own.wait()
+    everyone(arrived)
 
 
 def finish(n_all, values, sums, out, rms):

time: 27.5 us -> 27.3 us (level)
  no operation moved by 1% of the time
where the time goes in v4:
time: 27.3 us; the launch traced here: 27.1 us
  Pallas kernels  26.5 us (97%)
  between operations  0.64 us (2%)
    pallas_call x1, Pallas kernels, shards(): pl.pallas_call(functools.partial(kernel, n_outer, n_inner, chunks), out_s...  25.6 us
    pallas_call x1, Pallas kernels, shards(): pl.pallas_call(functools.partial(finish, n_all), out_shape=(jax.ShapeDtyp...  0.85 us

profile of v4, /device:TPU:0, one launch (start us, length us, event | category | flops | bytes accessed | tf_op | source)
XLA Modules:
  0.0 27.1 jit_solution(14795790693631831643)
XLA Ops:
  0.6 25.6 %shard_map.41 = (f32[2,2,128,128]{3,2,1,0:T(8,128)S(1)}, f32[32,1,128]{2,1,0:T(1,128)S(1)}) custom-call(f32[2,256,128]{2,1,0:T(8,128)} %bitcast.3, f32[4,2,128,128]{3,2,1,0:T(8,128)} %gates_in.1), custom_call_target="tpu_custom_call" | custom-call | tf_op jit(solution)/shard_map/pallas_call | solution.py:298
  26.3 0.8 %shard_map.42 = (f32[2,256,128]{2,1,0:T(8,128)}, f32[1,1]{1,0:T(1,128)}) custom-call(f32[2,2,128,128]{3,2,1,0:T(8,128)S(1)} %get-tuple-element.6.values, f32[32,1,128]{2,1,0:T(1,128)S(1)} %get-tuple-element.7.sums), custom_call_target="tpu_custom_call" | custom-call | tf_op jit(solution)/shard_map/pallas_call | solution.py:319

commit v5 on v4

--- a/solution.py
+++ b/solution.py
@@ -32,7 +32,8 @@
 
 
 def spread(position, count):
-    return (position % 2) * (count // 2) + position // 2
+    half, rest = count // 2, position // 2
+    return (position % 2) * half + (rest % 2) * (half // 2) + rest // 2
 
 
 def kernel(
@@ -276,10 +277,10 @@
     whole = jnp.sum(jnp.sum(sums[...], axis=0), axis=1, keepdims=True)
     root = jnp.sqrt(whole / (n_all * chunks * rows * dim))
     rms[...] = root
-    scale = jnp.broadcast_to(root, (8, dim))
+    scale = jnp.broadcast_to(1.0 / root, (8, dim))
     for chunk in range(chunks):
         for c in range(2):
-            scaled = values[chunk, c].reshape(-1, 8, dim) / scale[None]
+            scaled = values[chunk, c].reshape(-1, 8, dim) * scale[None]
             out[c, pl.ds(chunk, rows, stride=chunks), :] = scaled.reshape(-1, dim)
 
 

time: 27.3 us -> 26.7 us (0.978)
  Pallas kernels: 26.5 us -> 25.9 us
    pallas_call x1, Pallas kernels: 25.6 us -> 25.1 us  [shards(): pl.pallas_call(functools.partial(kernel, n_outer, n_inner, chunks), out_s...]
where the time goes in v5:
time: 26.7 us; the launch traced here: 26.6 us
  Pallas kernels  25.9 us (97%)
  between operations  0.64 us (2%)
    pallas_call x1, Pallas kernels, shards(): pl.pallas_call(functools.partial(kernel, n_outer, n_inner, chunks), out_s...  25.1 us
    pallas_call x1, Pallas kernels, shards(): pl.pallas_call(functools.partial(finish, n_all), out_shape=(jax.ShapeDtyp...  0.85 us

profile of v5, /device:TPU:0, one launch (start us, length us, event | category | flops | bytes accessed | tf_op | source)
XLA Modules:
  0.0 26.6 jit_solution(9027811969930617509)
XLA Ops:
  0.6 25.1 %shard_map.41 = (f32[2,2,128,128]{3,2,1,0:T(8,128)S(1)}, f32[32,1,128]{2,1,0:T(1,128)S(1)}) custom-call(f32[2,256,128]{2,1,0:T(8,128)} %bitcast.3, f32[4,2,128,128]{3,2,1,0:T(8,128)} %gates_in.1), custom_call_target="tpu_custom_call" | custom-call | tf_op jit(solution)/shard_map/pallas_call | solution.py:299
  25.7 0.8 %shard_map.42 = (f32[2,256,128]{2,1,0:T(8,128)}, f32[1,1]{1,0:T(1,128)}) custom-call(f32[2,2,128,128]{3,2,1,0:T(8,128)S(1)} %get-tuple-element.6.values, f32[32,1,128]{2,1,0:T(1,128)S(1)} %get-tuple-element.7.sums), custom_call_target="tpu_custom_call" | custom-call | tf_op jit(solution)/shard_map/pallas_call | solution.py:320

commit v6 on v5

--- a/solution.py
+++ b/solution.py
@@ -33,7 +33,7 @@
 
 def spread(position, count):
     half, rest = count // 2, position // 2
-    return (position % 2) * half + (rest % 2) * (half // 2) + rest // 2
+    return (rest % 2) * half + (position % 2) * (half // 2) + rest // 2
 
 
 def kernel(

time: 26.7 us -> 27.3 us (1.022)
  Pallas kernels: 25.9 us -> 26.5 us
    pallas_call x1, Pallas kernels: 25.1 us -> 25.7 us  [shards(): pl.pallas_call(functools.partial(kernel, n_outer, n_inner, chunks), out_s...]
where the time goes in v6:
time: 27.3 us; the launch traced here: 27.1 us
  Pallas kernels  26.5 us (97%)
  between operations  0.64 us (2%)
    pallas_call x1, Pallas kernels, shards(): pl.pallas_call(functools.partial(kernel, n_outer, n_inner, chunks), out_s...  25.7 us
    pallas_call x1, Pallas kernels, shards(): pl.pallas_call(functools.partial(finish, n_all), out_shape=(jax.ShapeDtyp...  0.85 us

profile of v6, /device:TPU:0, one launch (start us, length us, event | category | flops | bytes accessed | tf_op | source)
XLA Modules:
  0.0 27.1 jit_solution(8437060364503628372)
XLA Ops:
  0.6 25.7 %shard_map.41 = (f32[2,2,128,128]{3,2,1,0:T(8,128)S(1)}, f32[32,1,128]{2,1,0:T(1,128)S(1)}) custom-call(f32[2,256,128]{2,1,0:T(8,128)} %bitcast.3, f32[4,2,128,128]{3,2,1,0:T(8,128)} %gates_in.1), custom_call_target="tpu_custom_call" | custom-call | tf_op jit(solution)/shard_map/pallas_call | solution.py:299
  26.3 0.8 %shard_map.42 = (f32[2,256,128]{2,1,0:T(8,128)}, f32[1,1]{1,0:T(1,128)}) custom-call(f32[2,2,128,128]{3,2,1,0:T(8,128)S(1)} %get-tuple-element.6.values, f32[32,1,128]{2,1,0:T(1,128)S(1)} %get-tuple-element.7.sums), custom_call_target="tpu_custom_call" | custom-call | tf_op jit(solution)/shard_map/pallas_call | solution.py:320
